TPU v7x, 32 devices: a whole 2x2x4 slice. The times are simulated.
32 devices in a mesh: group: 8 (over y, x, core), tp: 4 (over z).
Axes of the slice: x: 2, y: 2, z: 4, core: 2. Of those that a mesh axis runs over, the one named last changes fastest.
Arguments:
- queries: bfloat16 [128, 8192], P('group', 'tp'), may hold values from -100 to 100
- cache_keys: bfloat16 [128, 512, 1024], P('group', None, 'tp'), may hold values from -6 to 6
- cache_values: bfloat16 [128, 512, 1024], P('group', None, 'tp'), may hold values from -6 to 6
- pool_keys: bfloat16 [16, 4096, 1024], P('group', None, 'tp'), may hold values from -6 to 6
- pool_values: bfloat16 [16, 4096, 1024], P('group', None, 'tp'), may hold values from -6 to 6
- row_lengths: int32 [128], P('group'), may hold values from 2 to 49664, as said below
- slot_owner: int32 [16], P('group'), may hold values from -1 to 127, as said below
- slot_fill: int32 [16], P('group'), may hold values from 0 to 4096, as said below
- free_counts: int32 [8], P('group'), may hold values from 0 to 2047
- out_weight: bfloat16 [8192, 8192], P('tp'), may hold values from -0.0625 to 0.0625
Outputs:
- mixed_out: bfloat16 [128, 8192], P('group', 'tp')
- total_free: int32 [1], replicated
Inputs may be any that keep to these rules, and one draw needn't show every extreme that they name: `row_lengths`: A row of length over 512 has the rest of its positions in the slots it owns, so its length is 512 plus the sum of their slot_fill; other rows own no slot. `slot_owner`: each slot is free or holds one block of one row; slots may sit in any group, the row's own too. `slot_fill`: A free slot has fill 0, an owned one at least 2.
All inputs are finite; a program needn't handle non-finite values.
Results may differ from a plain program's by a relative error of at most 0.0066.
Values may be sent and summed in bfloat16 or wider, within the bound.
No kernel may reach another device: no remote copies, remote signals or barrier semaphores. Data moves between devices by JAX's collectives and lax.ppermute only.
A program may use at most 128 MiB of HBM per device.

v0:
```python
import math

import jax
import jax.numpy as jnp
from jax import lax
from jax.experimental import pallas as pl
from jax.experimental.pallas import tpu as pltpu
from jax.sharding import PartitionSpec as P


HEAD_DIM = 128
LANES = 128
PARTS = 4
far_below = -1e30


VMEM = pl.BlockSpec(memory_space=pltpu.VMEM)
SMEM = pl.BlockSpec(memory_space=pltpu.SMEM)
HBM = pl.BlockSpec(memory_space=pltpu.MemorySpace.HBM)
f32 = jnp.float32
bf16 = jnp.bfloat16


def call(kernel, outs, ins, scratch=(), out_specs=None, flops=0, moved=0, vmem=8 << 20):
    return pl.pallas_call(
        kernel,
        out_shape=outs,
        in_specs=ins,
        out_specs=out_specs if out_specs is not None else jax.tree.map(lambda _: VMEM, outs),
        scratch_shapes=scratch,
        cost_estimate=pl.CostEstimate(flops=flops, bytes_accessed=moved, transcendentals=0),
        compiler_params=pltpu.CompilerParams(vmem_limit_bytes=vmem),
    )


def spread_heads(tile, kv_heads):
    if kv_heads == 1:
        return tile
    heads = tile.shape[0]
    owner = lax.broadcasted_iota(jnp.int32, tile.shape, 0) // (heads // kv_heads)
    return jnp.concatenate(
        [jnp.where(owner == k, tile, jnp.zeros_like(tile)) for k in range(kv_heads)], axis=1
    )


def own_columns(wide, kv_heads):
    if kv_heads == 1:
        return wide
    heads = wide.shape[0]
    owner = lax.broadcasted_iota(jnp.int32, (heads, HEAD_DIM), 0) // (heads // kv_heads)
    picked = wide[:, :HEAD_DIM]
    for k in range(1, kv_heads):
        picked = jnp.where(owner == k, wide[:, k * HEAD_DIM : (k + 1) * HEAD_DIM], picked)
    return picked


def scores_of(query, keys):
    return lax.dot_general(
        query, keys, (((1,), (1,)), ((), ())), preferred_element_type=f32
    ) * (math.log2(math.e) / math.sqrt(HEAD_DIM))


def open_kernel(_, token):
    token[...] = jnp.zeros_like(token)


def local_kernel(
    lengths, q_ref, keys, values, weight_in, _, packed, *rest,
    rows, heads, kv_heads, pieces, columns,
):
    q_heads, scores, weights, fetch_sems = rest[len(pieces) :]
    positions = keys.shape[1]
    weight_copies = fetch(weight_in, pieces, rest, fetch_sems, columns)

    @region
    def _():
        wide = q_ref[...].astype(f32)
        for h in range(heads):
            q_heads[pl.ds(h, rows, stride=heads), :] = wide[:, h * HEAD_DIM : (h + 1) * HEAD_DIM]

    place = lax.broadcasted_iota(jnp.int32, (heads, positions), 1)

    def score(r):
        query = spread_heads(q_heads[pl.ds(r * heads, heads), :].astype(bf16), kv_heads)
        scores[r] = jnp.where(place < lengths[r], scores_of(query, keys[r]), far_below)

    def weigh(r):
        high = jnp.max(scores[r], axis=-1, keepdims=True)
        weight = jnp.exp2(scores[r] - high)
        total = jnp.sum(weight, axis=-1, keepdims=True)
        weights[r] = weight.astype(bf16)
        for i, value in ((1, high), (2, total)):
            at = pl.ds((i * rows + r) * heads, heads)
            packed[at, :] = jnp.broadcast_to(value, (heads, LANES))

    def mix(r):
        mixed = jnp.dot(weights[r], values[r], preferred_element_type=f32)
        packed[pl.ds(r * heads, heads), :] = own_columns(mixed, kv_heads)

    @region
    def _():
        pipeline((score, weigh, mix), rows, 3)

    for copy in weight_copies:
        copy.wait()


def pipeline(stages, count, apart):
    for t in range(count + apart * (len(stages) - 1)):
        for k, stage in enumerate(stages):
            if 0 <= t - k * apart < count:
                stage(t - k * apart)


def step_mask(group, step):
    return 2 * step + group % 2


def piece_of(weight, piece, columns):
    step, part = piece
    place = jnp.bitwise_xor(lax.axis_index("tp"), step_mask(lax.axis_index("group"), step))
    depth = weight.shape[0] // PARTS
    return weight.at[
        pl.ds(part * depth, depth), pl.ds(pl.multiple_of(place * columns, columns), columns)
    ]


def fetch(weight, pieces, targets, sems, columns):
    copies = [
        pltpu.make_async_copy(piece_of(weight, piece, columns), target, sems.at[i])
        for i, (piece, target) in enumerate(zip(pieces, targets))
    ]

    for copy in copies:
        copy.start()
    return copies


def region(body):
    pl.when(lax.axis_index("group") >= 0)(body)


def fetch_kernel(weight, _, *rest, pieces, columns):
    for copy in fetch(weight, pieces, rest[:-1], rest[-1], columns):
        copy.wait()


def split_stats(stats):
    spread = jnp.zeros_like(stats)
    for i in range(3):
        term = stats.astype(bf16).astype(f32)
        stats = stats - term
        spread = spread + (pltpu.roll(term, i * LANES // 4, 1) if i else term)
    return spread.astype(bf16)


def join_stats(tile):
    spread = tile.astype(f32)
    return (
        spread + pltpu.roll(spread, 3 * LANES // 4, 1) + pltpu.roll(spread, 2 * LANES // 4, 1)
    )


def slot_kernel(*refs, groups, rows, heads, kv_heads, slots, chunk, pieces, columns):
    owners, fills, free = refs[:3]
    shards = refs[3 : 3 + groups]
    keys, values, weight_in = refs[3 + groups : 6 + groups]
    packed, *rest = refs[6 + groups :]
    q_heads, scores, weights, fetch_sems = rest[len(pieces) :]
    weight_copies = fetch(weight_in, pieces, rest, fetch_sems, columns)
    positions = keys.shape[1]
    me = lax.axis_index("group")
    row_at = lax.broadcasted_iota(jnp.int32, (rows, heads * HEAD_DIM), 0)
    for s in range(slots):
        owner = jnp.maximum(owners[s], 0)
        home = lax.div(owner, rows)
        row = lax.rem(owner, rows)
        for k in range(groups):

            @pl.when(jnp.bitwise_xor(home, me) == k)
            def _(k=k, s=s, row=row):
                block = jnp.where(row_at == row, shards[k][...].astype(f32), 0.0)
                single = jnp.sum(block, axis=0, keepdims=True)
                for h in range(heads):
                    q_heads[s * heads + h : s * heads + h + 1, :] = single[
                        :, h * HEAD_DIM : (h + 1) * HEAD_DIM
                    ]

    lane = lax.broadcasted_iota(jnp.int32, (heads, LANES), 1)
    stats = jnp.where(lane == 3 * slots, free[0].astype(f32), 0.0)
    places = lax.broadcasted_iota(jnp.int32, (heads, chunk), 1)
    queries = [
        spread_heads(q_heads[s * heads : (s + 1) * heads, :].astype(bf16), kv_heads)
        for s in range(slots)
    ]
    highs, bases = [None] * slots, [None] * slots
    totals, mixes = [0.0] * slots, [0.0] * slots
    steps = positions // chunk

    def score(s, c):
        at = pl.ds(c * chunk, chunk)
        found = jnp.where(
            places < fills[s] - c * chunk, scores_of(queries[s], keys[s, at, :]), far_below
        )
        scores[s, :, at] = found
        highs[s] = found if c == 0 else jnp.maximum(highs[s], found)
        if c == steps - 1:
            highs[s] = jnp.max(highs[s], axis=-1, keepdims=True)
            bases[s] = jnp.maximum(highs[s], far_below / 2)

    def weigh(s, c):
        at = pl.ds(c * chunk, chunk)
        weight = jnp.exp2(scores[s, :, at] - bases[s])
        totals[s] = totals[s] + weight
        weights[s, :, at] = weight.astype(bf16)

    def mix(s, c):
        at = pl.ds(c * chunk, chunk)
        mixes[s] = mixes[s] + jnp.dot(
            weights[s, :, at], values[s, at, :], preferred_element_type=f32
        )

    for t in range(slots + 2):
        for c in range(steps):
            for stage, s in ((score, t), (weigh, t - 1), (mix, t - 2)):
                if 0 <= s < slots:
                    stage(s, c)
    for s in range(slots):
        total = jnp.sum(totals[s], axis=-1, keepdims=True)
        packed[s * heads : (s + 1) * heads, :] = own_columns(mixes[s], kv_heads).astype(bf16)
        stats = jnp.where(lane == s, highs[s], stats)
        stats = jnp.where(lane == slots + s, total, stats)
        stats = jnp.where(lane == 2 * slots + s, owners[s].astype(f32), stats)
    packed[slots * heads :, :] = split_stats(stats)
    for copy in weight_copies:
        copy.wait()


def project(x, held, same, other, chunk, own=None):
    rows, depth = x.shape[0] // 2, x.shape[1] // PARTS
    for c in range(0, same.shape[1], chunk):
        at = slice(c, c + chunk)
        product = sum(
            jnp.dot(
                x[:, p * depth : (p + 1) * depth], held[p][:, at], preferred_element_type=f32
            )
            for p in range(PARTS)
        )
        same[:, at] = product[:rows].astype(same.dtype)
        other[:, at] = product[rows:].astype(other.dtype)
        if own is not None:
            own[:, at] = product[:rows]


def combine_kernel(*refs, groups, rows, heads, slots, pieces, last, columns, chunk):
    local, gathered = refs[:2], refs[2 : 2 + groups]
    held, refs = refs[2 + groups : 2 + groups + PARTS], refs[2 + groups + PARTS :]
    weight_in, x_ref, free_total, same, other, *rest = refs
    own = rest.pop(0) if last else None
    mixed, high, total, sems = rest[len(pieces) :]
    copies = fetch(weight_in, pieces, rest, sems, columns)

    @region
    def _():
        flat, each = rows * heads, (slots + 1) * heads
        me = lax.axis_index("group")
        first, second = me * rows, jnp.bitwise_xor(me, 1) * rows
        free = jnp.zeros((heads, LANES), f32)
        found = []
        for part in gathered:
            for k in range(0, part.shape[0], each):
                stats = join_stats(part[k + slots * heads : k + each, :])
                free = free + stats
                for s in range(slots):
                    owner = stats[0, 2 * slots + s].astype(jnp.int32)
                    found.append((part, k, s, stats, owner))
        free_total[0] = free[0, 3 * slots].astype(jnp.int32)
        for i in range(2):
            high[i * flat : (i + 1) * flat, :] = local[i][flat : 2 * flat, :]
        slot_stats = []
        for part, k, s, stats, owner in found:
            in_first = (owner >= first) & (owner < first + rows)
            in_second = (owner >= second) & (owner < second + rows)
            row = jnp.where(
                in_first, owner - first, jnp.where(in_second, owner - second + rows, 0)
            )
            mine = in_first | in_second
            at = pl.ds(pl.multiple_of(row * heads, heads), heads)
            slot_high = jnp.broadcast_to(stats[:, s : s + 1], (heads, LANES))
            slot_total = jnp.broadcast_to(stats[:, slots + s : slots + s + 1], (heads, LANES))
            slot_stats.append((part, k + s * heads, mine, at, slot_high, slot_total))
            high[at, :] = jnp.maximum(high[at, :], jnp.where(mine, slot_high, far_below))
        for i in range(2):
            at = slice(i * flat, (i + 1) * flat)
            keep = jnp.exp2(local[i][flat : 2 * flat, :] - high[at, :])
            mixed[at, :] = keep * local[i][:flat, :]
            total[at, :] = keep * local[i][2 * flat :, :]
        for part, k, mine, at, slot_high, slot_total in slot_stats:
            add = jnp.where(mine, jnp.exp2(jnp.minimum(slot_high - high[at, :], 0.0)), 0.0)
            mixed[at, :] = mixed[at, :] + add * part[k : k + heads, :].astype(f32)
            total[at, :] = total[at, :] + add * slot_total
        mixed[...] = mixed[...] / total[...]
        for h in range(heads):
            x_ref[:, h * HEAD_DIM : (h + 1) * HEAD_DIM] = mixed[
                pl.ds(h, 2 * rows, stride=heads), :
            ].astype(bf16)

    @region
    def _():
        project(x_ref[...], held, same, other, chunk, own)

    for copy in copies:
        copy.wait()


def project_kernel(x_ref, *refs, pieces, last, columns, chunk):
    held = refs[:PARTS]
    weight_in, same, other, *rest = refs[PARTS:]
    own = rest.pop(0) if last else None
    copies = fetch(weight_in, pieces, rest, rest[-1], columns)
    region(lambda: project(x_ref[...], held, same, other, chunk, own))
    for copy in copies:
        copy.wait()


def pick_kernel(even, odd, out):
    first = lax.axis_index("group") % 2 == 0

    @pl.when(first)
    def _():
        out[...] = even[...]

    @pl.when(jnp.logical_not(first))
    def _():
        out[...] = odd[...]


def sum_kernel(own, crossed, *refs):
    total = jnp.where(lax.axis_index("group") % 2 == 0, own[...], crossed[...].astype(f32))
    for part in refs[:-1]:
        total = total + part[...].astype(f32)
    refs[-1][...] = total.astype(bf16)


def send_block(value, step, crossed):
    groups, tp = lax.axis_size("group"), lax.axis_size("tp")
    pairs = [
        (g * tp + z, g * tp + (z ^ step_mask(g ^ crossed, step)))
        for g in range(groups)
        for z in range(tp)
    ]
    return lax.ppermute(value, ("group", "tp"), pairs)


def swap(value, axis, mask):
    size = lax.axis_size(axis)
    return lax.ppermute(value, axis, [(i, i ^ mask) for i in range(size)])


def gather_group(value):
    groups = lax.axis_size("group")
    found = [None] * groups
    found[0] = value
    found[1] = swap(value, "group", 1)
    for k in range(2, groups, 2):
        found[k] = swap(value, "group", k)
    for k in range(2, groups, 2):
        found[k + 1] = swap(found[k], "group", 1)
    return found


def step(
    queries,
    cache_keys,
    cache_values,
    pool_keys,
    pool_values,
    row_lengths,
    slot_owner,
    slot_fill,
    free_counts,
    out_weight,
):
    groups, tp = lax.axis_size("group"), lax.axis_size("tp")
    rows, width = queries.shape
    heads = width // HEAD_DIM
    kv_heads = cache_keys.shape[2] // HEAD_DIM
    slots, positions = pool_keys.shape[:2]
    columns = out_weight.shape[1] // tp
    chunk = math.gcd(columns, 512)
    sizes = dict(rows=rows, heads=heads)

    shards = gather_group(queries)
    out_weight = pltpu.with_memory_space_constraint(out_weight, pltpu.MemorySpace.HBM)
    copies = pltpu.SemaphoreType.DMA

    order = list(range(tp // 2 - 1, -1, -1))
    pieces = [(step, part) for step in order for part in range(PARTS)]
    held = jax.ShapeDtypeStruct((width // PARTS, columns), out_weight.dtype)
    piece_bytes = 2 * width * columns // PARTS
    weights = {}

    def take(count):
        taken = pieces[:count]
        del pieces[:count]
        return taken

    token = call(open_kernel, jax.ShapeDtypeStruct((8, LANES), f32), [HBM], vmem=1 << 20)(
        out_weight
    )
    taken = take(0)
    local, *more = call(
        lambda *refs, taken=taken: local_kernel(
            *refs, kv_heads=kv_heads, pieces=taken, columns=columns, **sizes
        ),
        [
            jax.ShapeDtypeStruct((3 * rows * heads, LANES), f32),
        ]
        + [held] * len(taken),
        [SMEM, VMEM, VMEM, VMEM, HBM, VMEM],
        scratch=[
            pltpu.VMEM((rows * heads, HEAD_DIM), f32),
            pltpu.VMEM((rows, heads, cache_keys.shape[1]), f32),
            pltpu.VMEM((rows, heads, cache_keys.shape[1]), bf16),
            copies((1,)),
        ],
        moved=2 * (cache_keys.size + cache_values.size),
        vmem=4 << 20,
    )(row_lengths, queries, cache_keys, cache_values, out_weight, token)
    weights.update(zip(taken, more))
    pair_local = swap(local, "group", 1)

    taken = take(3)
    packed, *more = call(
        lambda *refs, taken=taken: slot_kernel(
            *refs,
            groups=groups,
            kv_heads=kv_heads,
            slots=slots,
            chunk=math.gcd(positions, 512),
            pieces=taken,
            columns=columns,
            **sizes,
        ),
        [jax.ShapeDtypeStruct(((slots + 1) * heads, LANES), bf16)] + [held] * len(taken),
        [SMEM] * 3 + [VMEM] * (groups + 2) + [HBM],
        scratch=[
            pltpu.VMEM((slots * heads, HEAD_DIM), f32),
            pltpu.VMEM((slots, heads, positions), f32),
            pltpu.VMEM((slots, heads, positions), bf16),
            copies((len(taken),)),
        ],
        moved=2 * (pool_keys.size + pool_values.size),
        vmem=4 << 20,
    )(slot_owner, slot_fill, free_counts, *shards, pool_keys, pool_values, out_weight)
    weights.update(zip(taken, more))

    far = gather_group(packed)
    taken = take(2)
    more = call(
        lambda *refs, taken=taken: fetch_kernel(*refs, pieces=taken, columns=columns),
        [held] * len(taken),
        [HBM, pl.BlockSpec(memory_space=pl.ANY)],
        scratch=[copies((len(taken),))],
        moved=piece_bytes * len(taken),
        vmem=1 << 20,
    )(out_weight, packed)
    weights.update(zip(taken, more))

    block = jax.ShapeDtypeStruct((rows, columns), bf16)
    whole = jax.ShapeDtypeStruct((rows, columns), f32)
    received = []
    for i, step in enumerate(order):
        last = step == 0
        taken = take(max(0, len(pieces) - PARTS * (len(order) - 2 - i)))
        outs = [block] * 2 + [whole] * last + [held] * len(taken)
        settings = dict(pieces=taken, last=last, columns=columns, chunk=chunk)
        ready = [weights[step, part] for part in range(PARTS)]
        moved = piece_bytes * max(PARTS, len(taken))
        if i == 0:
            x, free_total, same, other, *more = call(
                lambda *refs: combine_kernel(
                    *refs, groups=groups, slots=slots, **settings, **sizes
                ),
                [
                    jax.ShapeDtypeStruct((2 * rows, width), bf16),
                    jax.ShapeDtypeStruct((1,), jnp.int32),
                ]
                + outs,
                [VMEM] * (2 + groups + PARTS) + [HBM],
                out_specs=[VMEM, SMEM] + [VMEM] * len(outs),
                scratch=[pltpu.VMEM((2 * rows * heads, LANES), f32)] * 3
                + [copies((max(1, len(taken)),))],
                moved=moved,
            )(local, pair_local, *far, *ready, out_weight)
        else:
            same, other, *more = call(
                lambda *refs, settings=settings: project_kernel(*refs, **settings),
                outs,
                [VMEM] * (1 + PARTS) + [HBM],
                scratch=[copies((max(1, len(taken)),))],
                moved=moved,
                vmem=4 << 20,
            )(x, *ready, out_weight)
        if last:
            own = more.pop(0)
        weights.update(zip(taken, more))
        crossed = swap(other, "group", 1)
        if last:
            leaving = call(pick_kernel, block, [VMEM] * 2, vmem=1 << 20)(crossed, same)
            received.append(swap(leaving, "tp", 1))
        else:
            received.append(send_block(same, step, 0))
            received.append(send_block(crossed, step, 1))
    mixed_out = call(sum_kernel, block, [VMEM] * (2 + len(received)))(own, crossed, *received)
    return (mixed_out, free_total)


def solution(mesh):
    in_specs = (
        P("group", "tp"),
        P("group", None, "tp"),
        P("group", None, "tp"),
        P("group", None, "tp"),
        P("group", None, "tp"),
        P("group"),
        P("group"),
        P("group"),
        P("group"),
        P("tp", None),
    )
    out_specs = (P("group", "tp"), P())
    return jax.shard_map(step, mesh=mesh, in_specs=in_specs, out_specs=out_specs, check_vma=False)
```

profile of v0, /device:TPU:0, one launch (start us, length us, event | category | flops | bytes accessed | tf_op | source)
XLA Modules:
  0.0 45.9 jit_solution(1707916467437266248)
XLA Ops:
  0.7 0.8 %copy-done.4 = bf16[16,2048]{1,0:T(8,128)(2,1)S(1)} copy-done((bf16[16,2048]{1,0:T(8,128)(2,1)S(1)}, bf16[16,2048]{1,0:T(8,128)(2,1)}, u32[]{:S(2)}) %copy-start.4) | copy-done | bytes 65560
  1.5 1.4 %copy-done = bf16[16,512,256]{2,1,0:T(8,128)(2,1)S(1)} copy-done((bf16[16,512,256]{2,1,0:T(8,128)(2,1)S(1)}, bf16[16,512,256]{2,1,0:T(8,128)(2,1)}, u32[]{:S(2)}) %copy-start) | copy-done | bytes 4194328
  2.9 1.3 %copy-done.1 = bf16[16,512,256]{2,1,0:T(8,128)(2,1)S(1)} copy-done((bf16[16,512,256]{2,1,0:T(8,128)(2,1)S(1)}, bf16[16,512,256]{2,1,0:T(8,128)(2,1)}, u32[]{:S(2)}) %copy-start.1) | copy-done | bytes 4194328
  4.2 2.4 %shard_map.114.refs_0_ = f32[768,128]{1,0:T(8,128)S(1)} custom-call(s32[16]{0:T(128)S(1)} %copy-done.5, bf16[16,2048]{1,0:T(8,128)(2,1)S(1)} %copy-done.4, bf16[16,512,256]{2,1,0:T(8,128)(2,1)S(1)} %copy-done, bf16[16,512,256]{2,1,0:T(8,128)(2,1)S(1)} %copy-done.1, bf16[2048,8192]{1,0:T(8,128)(2,1)} %refs_5_.1, f32[8,128]{1,0:T(8,128)S(1)} %shard_map.113.refs_5_), custom_call_target="tpu_custom_call" | custom-call | bytes 8388608 | tf_op jit(solution)/shard_map/pallas_call | solution.py:412
  7.1 2.6 %collective-permute-start.4 = (bf16[16,2048]{1,0:T(8,128)(2,1)S(1)}, bf16[16,2048]{1,0:T(8,128)(2,1)S(1)}, u32[]{:S(2)}, u32[]{:S(2)}) collective-permute-start(bf16[16,2048]{1,0:T(8,128)(2,1)S(1)} %copy-done.4), channel_id=1, source_target_pairs={{0,16},{4,20},{8,24},{12,28},{16,0},{20,4},{24,8},{28,12},{1,17},{... | collective-permute-start | bytes 196616 | tf_op jit(solution)/shard_map/ppermute | solution.py:357
  9.7 1.5 %collective-permute-start.2 = (bf16[16,2048]{1,0:T(8,128)(2,1)S(1)}, bf16[16,2048]{1,0:T(8,128)(2,1)S(1)}, u32[]{:S(2)}, u32[]{:S(2)}) collective-permute-start(bf16[16,2048]{1,0:T(8,128)(2,1)S(1)} %copy-done.4), channel_id=1, source_target_pairs={{0,8},{4,12},{8,0},{12,4},{16,24},{20,28},{24,16},{28,20},{1,9},{5... | collective-permute-start | bytes 196616 | tf_op jit(solution)/shard_map/ppermute | solution.py:357
  11.3 1.1 %collective-permute-done.4.refs_7_ = bf16[16,2048]{1,0:T(8,128)(2,1)S(1)} collective-permute-done((bf16[16,2048]{1,0:T(8,128)(2,1)S(1)}, bf16[16,2048]{1,0:T(8,128)(2,1)S(1)}, u32[]{:S(2)}, u32[]{:S(2)}) %collective-permute-start.4) | collective-permute-done | bytes 65568 | tf_op jit(solution)/shard_map/ppermute | solution.py:357
  12.4 1.9 %collective-permute-done.2.refs_5_ = bf16[16,2048]{1,0:T(8,128)(2,1)S(1)} collective-permute-done((bf16[16,2048]{1,0:T(8,128)(2,1)S(1)}, bf16[16,2048]{1,0:T(8,128)(2,1)S(1)}, u32[]{:S(2)}, u32[]{:S(2)}) %collective-permute-start.2) | collective-permute-done | bytes 65568 | tf_op jit(solution)/shard_map/ppermute | solution.py:357
  14.3 2.0 %collective-permute-done.6.refs_9_ = bf16[16,2048]{1,0:T(8,128)(2,1)S(1)} collective-permute-done((bf16[16,2048]{1,0:T(8,128)(2,1)S(1)}, bf16[16,2048]{1,0:T(8,128)(2,1)S(1)}, u32[]{:S(2)}, u32[]{:S(2)}) %collective-permute-start.6) | collective-permute-done | bytes 65568 | tf_op jit(solution)/shard_map/ppermute | solution.py:357
  17.6 3.5 %shard_map.115 = (bf16[48,128]{1,0:T(8,128)(2,1)S(1)}, bf16[512,2048]{1,0:T(8,128)(2,1)S(1)}, bf16[512,2048]{1,0:T(8,128)(2,1)S(1)}, bf16[512,2048]{1,0:T(8,128)(2,1)S(1)}) custom-call(s32[2]{0:T(128)S(1)} %copy-done.6, s32[2]{0:T(128)S(1)} %copy-done.7, s32[1]{0:T(128)S(6)} %copy.12.refs_2_, bf16[16,2048]{1,0:T(8,128)(2,1)S(1)} %copy-done.4, ...), custom_call_target="tpu_custom_call" | custom-call | bytes 8388608 | tf_op jit(solution)/shard_map/pallas_call | solution.py:434
  21.1 1.4 %collective-permute-start.13 = (bf16[48,128]{1,0:T(8,128)(2,1)S(1)}, bf16[48,128]{1,0:T(8,128)(2,1)S(1)}, u32[]{:S(2)}, u32[]{:S(2)}) collective-permute-start(bf16[48,128]{1,0:T(8,128)(2,1)S(1)} %get-tuple-element.18.refs_1_.refs_2_), channel_id=1, source_target_pairs={{0,24},{4,28},{8,16},{12,20},{16,8},{20,12},{24,0},{28,4},{1,25},{... | collective-permute-start | bytes 36872 | tf_op jit(solution)/shard_map/ppermute | solution.py:357
  22.5 0.7 %collective-permute-start.11 = (bf16[48,128]{1,0:T(8,128)(2,1)S(1)}, bf16[48,128]{1,0:T(8,128)(2,1)S(1)}, u32[]{:S(2)}, u32[]{:S(2)}) collective-permute-start(bf16[48,128]{1,0:T(8,128)(2,1)S(1)} %get-tuple-element.18.refs_1_.refs_2_), channel_id=1, source_target_pairs={{0,16},{4,20},{8,24},{12,28},{16,0},{20,4},{24,8},{28,12},{1,17},{... | collective-permute-start | bytes 36872 | tf_op jit(solution)/shard_map/ppermute | solution.py:357
  23.2 1.5 %collective-permute-start.9 = (bf16[48,128]{1,0:T(8,128)(2,1)S(1)}, bf16[48,128]{1,0:T(8,128)(2,1)S(1)}, u32[]{:S(2)}, u32[]{:S(2)}) collective-permute-start(bf16[48,128]{1,0:T(8,128)(2,1)S(1)} %get-tuple-element.18.refs_1_.refs_2_), channel_id=1, source_target_pairs={{0,8},{4,12},{8,0},{12,4},{16,24},{20,28},{24,16},{28,20},{1,9},{5... | collective-permute-start | bytes 36872 | tf_op jit(solution)/shard_map/ppermute | solution.py:357
  24.7 1.1 %collective-permute-done.13.refs_8_ = bf16[48,128]{1,0:T(8,128)(2,1)S(1)} collective-permute-done((bf16[48,128]{1,0:T(8,128)(2,1)S(1)}, bf16[48,128]{1,0:T(8,128)(2,1)S(1)}, u32[]{:S(2)}, u32[]{:S(2)}) %collective-permute-start.13) | collective-permute-done | bytes 12320 | tf_op jit(solution)/shard_map/ppermute | solution.py:357
  26.9 2.2 %shard_map.116 = (bf16[512,2048]{1,0:T(8,128)(2,1)S(1)}, bf16[512,2048]{1,0:T(8,128)(2,1)S(1)}) custom-call(bf16[2048,8192]{1,0:T(8,128)(2,1)} %refs_5_.1, bf16[48,128]{1,0:T(8,128)(2,1)S(1)} %get-tuple-element.18.refs_1_.refs_2_), custom_call_target="tpu_custom_call" | custom-call | bytes 4194304 | tf_op jit(solution)/shard_map/pallas_call | solution.py:460
  29.2 3.4 %shard_map.117 = (bf16[32,2048]{1,0:T(8,128)(2,1)S(1)}, s32[1]{0:T(128)}, bf16[16,2048]{1,0:T(8,128)(2,1)S(1)}, bf16[16,2048]{1,0:T(8,128)(2,1)S(1)}, bf16[512,2...) custom-call(f32[768,128]{1,0:T(8,128)S(1)} %shard_map.114.refs_0_, ...), custom_call_target="tpu_custom_call" | custom-call | bytes 8388608 | tf_op jit(solution)/shard_map/pallas_call | solution.py:481
  32.6 1.6 %shard_map.118 = (bf16[16,2048]{1,0:T(8,128)(2,1)S(1)}, bf16[16,2048]{1,0:T(8,128)(2,1)S(1)}, f32[16,2048]{1,0:T(8,128)S(1)}) custom-call(bf16[32,2048]{1,0:T(8,128)(2,1)S(1)} %get-tuple-element.23.refs_0_, bf16[512,2048]{1,0:T(8,128)(2,1)S(1)} %get-tuple-element.24.refs_1_, bf16[512,2048]{1,0:T(8,128)(2,1)S(1)} %get-tuple-element.25.refs_2_, ...), custom_call_target="tpu_custom_call" | custom-call | bytes 8388608 | tf_op jit(solution)/shard_map/pallas_call | solution.py:497
  34.9 2.6 %collective-permute-start.16 = (bf16[16,2048]{1,0:T(8,128)(2,1)S(1)}, bf16[16,2048]{1,0:T(8,128)(2,1)S(1)}, u32[]{:S(2)}, u32[]{:S(2)}) collective-permute-start(bf16[16,2048]{1,0:T(8,128)(2,1)S(1)} %get-tuple-element.30), channel_id=1, source_target_pairs={{0,2},{1,3},{2,0},{3,1},{4,7},{5,6},{6,5},{7,4},{8,10},{9,11},{10,... | collective-permute-start | bytes 196616 | tf_op jit(solution)/shard_map/ppermute | solution.py:352
  37.5 1.6 %collective-permute-start.19 = (bf16[16,2048]{1,0:T(8,128)(2,1)S(1)}, bf16[16,2048]{1,0:T(8,128)(2,1)S(1)}, u32[]{:S(2)}, u32[]{:S(2)}) collective-permute-start(bf16[16,2048]{1,0:T(8,128)(2,1)S(1)} %shard_map.119), channel_id=1, source_target_pairs={{0,1},{1,0},{2,3},{3,2},{4,5},{5,4},{6,7},{7,6},{8,9},{9,8},{10,11... | collective-permute-start | bytes 196616 | tf_op jit(solution)/shard_map/ppermute | solution.py:357
  39.1 0.6 %collective-permute-start.18 = (bf16[16,2048]{1,0:T(8,128)(2,1)S(1)}, bf16[16,2048]{1,0:T(8,128)(2,1)S(1)}, u32[]{:S(2)}, u32[]{:S(2)}) collective-permute-start(bf16[16,2048]{1,0:T(8,128)(2,1)S(1)} %collective-permute-done.17), channel_id=1, source_target_pairs={{0,3},{1,2},{2,1},{3,0},{4,6},{5,7},{6,4},{7,5},{8,11},{9,10},{10,... | collective-permute-start | bytes 196616 | tf_op jit(solution)/shard_map/ppermute | solution.py:352
  39.8 2.1 %collective-permute-done.16.refs_0_ = bf16[16,2048]{1,0:T(8,128)(2,1)S(1)} collective-permute-done((bf16[16,2048]{1,0:T(8,128)(2,1)S(1)}, bf16[16,2048]{1,0:T(8,128)(2,1)S(1)}, u32[]{:S(2)}, u32[]{:S(2)}) %collective-permute-start.16) | collective-permute-done | bytes 65568 | tf_op jit(solution)/shard_map/ppermute | solution.py:352
  41.8 1.6 %collective-permute-done.19.refs_2_ = bf16[16,2048]{1,0:T(8,128)(2,1)S(1)} collective-permute-done((bf16[16,2048]{1,0:T(8,128)(2,1)S(1)}, bf16[16,2048]{1,0:T(8,128)(2,1)S(1)}, u32[]{:S(2)}, u32[]{:S(2)}) %collective-permute-start.19) | collective-permute-done | bytes 65568 | tf_op jit(solution)/shard_map/ppermute | solution.py:357
  43.4 1.7 %collective-permute-done.18.refs_1_ = bf16[16,2048]{1,0:T(8,128)(2,1)S(1)} collective-permute-done((bf16[16,2048]{1,0:T(8,128)(2,1)S(1)}, bf16[16,2048]{1,0:T(8,128)(2,1)S(1)}, u32[]{:S(2)}, u32[]{:S(2)}) %collective-permute-start.18) | collective-permute-done | bytes 65568 | tf_op jit(solution)/shard_map/ppermute | solution.py:352
  45.2 0.7 %shard_map.120 = bf16[16,2048]{1,0:T(8,128)(2,1)} custom-call(f32[16,2048]{1,0:T(8,128)S(1)} %get-tuple-element.28.own, bf16[16,2048]{1,0:T(8,128)(2,1)S(1)} %collective-permute-done.15.even.crossed, bf16[16,2048]{1,0:T(8,128)(2,1)S(1)} %collective-permute-done.16.refs_0_, bf16[16,2048]{1,0:T(8,128)(2,1)S(1)} %collective-permute-done.18.refs_1_, ...), custom_call_target="tpu_custom_call" | custom-call | tf_op jit(solution)/shard_map/pallas_call | solution.py:515
  (40 shorter events, 3.0 us)
Async XLA Ops:
  4.1 13.5 %copy-start.2 = (bf16[2,4096,256]{2,1,0:T(8,128)(2,1)S(1)}, bf16[2,4096,256]{2,1,0:T(8,128)(2,1)}, u32[]{:S(2)}) copy-start(bf16[2,4096,256]{2,1,0:T(8,128)(2,1)} %refs_11_.1) | copy-start | bytes 12582916
  4.1 13.5 %copy-start.3 = (bf16[2,4096,256]{2,1,0:T(8,128)(2,1)S(1)}, bf16[2,4096,256]{2,1,0:T(8,128)(2,1)}, u32[]{:S(2)}) copy-start(bf16[2,4096,256]{2,1,0:T(8,128)(2,1)} %refs_12_.1) | copy-start | bytes 12582916
  4.2 13.5 %copy-start.6 = (s32[2]{0:T(128)S(1)}, s32[2]{0:T(128)}, u32[]{:S(2)}) copy-start(s32[2]{0:T(128)} %refs_0_.4) | copy-start | bytes 28
  4.2 13.5 %copy-start.7 = (s32[2]{0:T(128)S(1)}, s32[2]{0:T(128)}, u32[]{:S(2)}) copy-start(s32[2]{0:T(128)} %refs_1_.3) | copy-start | bytes 28
  6.6 22.6 %collective-permute-start = (f32[768,128]{1,0:T(8,128)S(1)}, f32[768,128]{1,0:T(8,128)S(1)}, u32[]{:S(2)}, u32[]{:S(2)}) collective-permute-start(f32[768,128]{1,0:T(8,128)S(1)} %shard_map.114.refs_0_), channel_id=1, source_target_pairs={{0,4},{4,0},{8,12},{12,8},{16,20},{20,16},{24,28},{28,24},{1,5},{5... | collective-permute-start | bytes 1179656 | tf_op jit(solution)/shard_map/ppermute | solution.py:357
  7.1 5.3 %collective-permute-start.4 = (bf16[16,2048]{1,0:T(8,128)(2,1)S(1)}, bf16[16,2048]{1,0:T(8,128)(2,1)S(1)}, u32[]{:S(2)}, u32[]{:S(2)}) collective-permute-start(bf16[16,2048]{1,0:T(8,128)(2,1)S(1)} %copy-done.4), channel_id=1, source_target_pairs={{0,16},{4,20},{8,24},{12,28},{16,0},{20,4},{24,8},{28,12},{1,17},{... | collective-permute-start | bytes 196616 | tf_op jit(solution)/shard_map/ppermute | solution.py:357
  9.7 4.6 %collective-permute-start.2 = (bf16[16,2048]{1,0:T(8,128)(2,1)S(1)}, bf16[16,2048]{1,0:T(8,128)(2,1)S(1)}, u32[]{:S(2)}, u32[]{:S(2)}) collective-permute-start(bf16[16,2048]{1,0:T(8,128)(2,1)S(1)} %copy-done.4), channel_id=1, source_target_pairs={{0,8},{4,12},{8,0},{12,4},{16,24},{20,28},{24,16},{28,20},{1,9},{5... | collective-permute-start | bytes 196616 | tf_op jit(solution)/shard_map/ppermute | solution.py:357
  11.2 5.2 %collective-permute-start.6 = (bf16[16,2048]{1,0:T(8,128)(2,1)S(1)}, bf16[16,2048]{1,0:T(8,128)(2,1)S(1)}, u32[]{:S(2)}, u32[]{:S(2)}) collective-permute-start(bf16[16,2048]{1,0:T(8,128)(2,1)S(1)} %copy-done.4), channel_id=1, source_target_pairs={{0,24},{4,28},{8,16},{12,20},{16,8},{20,12},{24,0},{28,4},{1,25},{... | collective-permute-start | bytes 196616 | tf_op jit(solution)/shard_map/ppermute | solution.py:357
  11.3 5.8 %collective-permute-start.1 = (bf16[16,2048]{1,0:T(8,128)(2,1)S(1)}, bf16[16,2048]{1,0:T(8,128)(2,1)S(1)}, u32[]{:S(2)}, u32[]{:S(2)}) collective-permute-start(bf16[16,2048]{1,0:T(8,128)(2,1)S(1)} %copy-done.4), channel_id=1, source_target_pairs={{0,4},{4,0},{8,12},{12,8},{16,20},{20,16},{24,28},{28,24},{1,5},{5... | collective-permute-start | bytes 196616 | tf_op jit(solution)/shard_map/ppermute | solution.py:357
  12.4 4.6 %collective-permute-start.5 = (bf16[16,2048]{1,0:T(8,128)(2,1)S(1)}, bf16[16,2048]{1,0:T(8,128)(2,1)S(1)}, u32[]{:S(2)}, u32[]{:S(2)}) collective-permute-start(bf16[16,2048]{1,0:T(8,128)(2,1)S(1)} %collective-permute-done.4.refs_7_), channel_id=1, source_target_pairs={{0,4},{4,0},{8,12},{12,8},{16,20},{20,16},{24,28},{28,24},{1,5},{5... | collective-permute-start | bytes 196616 | tf_op jit(solution)/shard_map/ppermute | solution.py:357
  14.3 2.7 %collective-permute-start.3 = (bf16[16,2048]{1,0:T(8,128)(2,1)S(1)}, bf16[16,2048]{1,0:T(8,128)(2,1)S(1)}, u32[]{:S(2)}, u32[]{:S(2)}) collective-permute-start(bf16[16,2048]{1,0:T(8,128)(2,1)S(1)} %collective-permute-done.2.refs_5_), channel_id=1, source_target_pairs={{0,4},{4,0},{8,12},{12,8},{16,20},{20,16},{24,28},{28,24},{1,5},{5... | collective-permute-start | bytes 196616 | tf_op jit(solution)/shard_map/ppermute | solution.py:357
  16.4 1.3 %collective-permute-start.7 = (bf16[16,2048]{1,0:T(8,128)(2,1)S(1)}, bf16[16,2048]{1,0:T(8,128)(2,1)S(1)}, u32[]{:S(2)}, u32[]{:S(2)}) collective-permute-start(bf16[16,2048]{1,0:T(8,128)(2,1)S(1)} %collective-permute-done.6.refs_9_), channel_id=1, source_target_pairs={{0,4},{4,0},{8,12},{12,8},{16,20},{20,16},{24,28},{28,24},{1,5},{5... | collective-permute-start | bytes 196616 | tf_op jit(solution)/shard_map/ppermute | solution.py:357
  21.1 4.7 %collective-permute-start.13 = (bf16[48,128]{1,0:T(8,128)(2,1)S(1)}, bf16[48,128]{1,0:T(8,128)(2,1)S(1)}, u32[]{:S(2)}, u32[]{:S(2)}) collective-permute-start(bf16[48,128]{1,0:T(8,128)(2,1)S(1)} %get-tuple-element.18.refs_1_.refs_2_), channel_id=1, source_target_pairs={{0,24},{4,28},{8,16},{12,20},{16,8},{20,12},{24,0},{28,4},{1,25},{... | collective-permute-start | bytes 36872 | tf_op jit(solution)/shard_map/ppermute | solution.py:357
  22.5 3.7 %collective-permute-start.11 = (bf16[48,128]{1,0:T(8,128)(2,1)S(1)}, bf16[48,128]{1,0:T(8,128)(2,1)S(1)}, u32[]{:S(2)}, u32[]{:S(2)}) collective-permute-start(bf16[48,128]{1,0:T(8,128)(2,1)S(1)} %get-tuple-element.18.refs_1_.refs_2_), channel_id=1, source_target_pairs={{0,16},{4,20},{8,24},{12,28},{16,0},{20,4},{24,8},{28,12},{1,17},{... | collective-permute-start | bytes 36872 | tf_op jit(solution)/shard_map/ppermute | solution.py:357
  23.2 3.7 %collective-permute-start.9 = (bf16[48,128]{1,0:T(8,128)(2,1)S(1)}, bf16[48,128]{1,0:T(8,128)(2,1)S(1)}, u32[]{:S(2)}, u32[]{:S(2)}) collective-permute-start(bf16[48,128]{1,0:T(8,128)(2,1)S(1)} %get-tuple-element.18.refs_1_.refs_2_), channel_id=1, source_target_pairs={{0,8},{4,12},{8,0},{12,4},{16,24},{20,28},{24,16},{28,20},{1,9},{5... | collective-permute-start | bytes 36872 | tf_op jit(solution)/shard_map/ppermute | solution.py:357
  24.7 4.5 %collective-permute-start.8 = (bf16[48,128]{1,0:T(8,128)(2,1)S(1)}, bf16[48,128]{1,0:T(8,128)(2,1)S(1)}, u32[]{:S(2)}, u32[]{:S(2)}) collective-permute-start(bf16[48,128]{1,0:T(8,128)(2,1)S(1)} %get-tuple-element.18.refs_1_.refs_2_), channel_id=1, source_target_pairs={{0,4},{4,0},{8,12},{12,8},{16,20},{20,16},{24,28},{28,24},{1,5},{5... | collective-permute-start | bytes 36872 | tf_op jit(solution)/shard_map/ppermute | solution.py:357
  25.8 3.4 %collective-permute-start.14 = (bf16[48,128]{1,0:T(8,128)(2,1)S(1)}, bf16[48,128]{1,0:T(8,128)(2,1)S(1)}, u32[]{:S(2)}, u32[]{:S(2)}) collective-permute-start(bf16[48,128]{1,0:T(8,128)(2,1)S(1)} %collective-permute-done.13.refs_8_), channel_id=1, source_target_pairs={{0,4},{4,0},{8,12},{12,8},{16,20},{20,16},{24,28},{28,24},{1,5},{5... | collective-permute-start | bytes 36872 | tf_op jit(solution)/shard_map/ppermute | solution.py:357
  26.2 3.0 %collective-permute-start.12 = (bf16[48,128]{1,0:T(8,128)(2,1)S(1)}, bf16[48,128]{1,0:T(8,128)(2,1)S(1)}, u32[]{:S(2)}, u32[]{:S(2)}) collective-permute-start(bf16[48,128]{1,0:T(8,128)(2,1)S(1)} %collective-permute-done.11.refs_6_), channel_id=1, source_target_pairs={{0,4},{4,0},{8,12},{12,8},{16,20},{20,16},{24,28},{28,24},{1,5},{5... | collective-permute-start | bytes 36872 | tf_op jit(solution)/shard_map/ppermute | solution.py:357
  26.9 2.3 %collective-permute-start.10 = (bf16[48,128]{1,0:T(8,128)(2,1)S(1)}, bf16[48,128]{1,0:T(8,128)(2,1)S(1)}, u32[]{:S(2)}, u32[]{:S(2)}) collective-permute-start(bf16[48,128]{1,0:T(8,128)(2,1)S(1)} %collective-permute-done.9.refs_4_), channel_id=1, source_target_pairs={{0,4},{4,0},{8,12},{12,8},{16,20},{20,16},{24,28},{28,24},{1,5},{5... | collective-permute-start | bytes 36872 | tf_op jit(solution)/shard_map/ppermute | solution.py:357
  34.2 3.2 %collective-permute-start.15 = (bf16[16,2048]{1,0:T(8,128)(2,1)S(1)}, bf16[16,2048]{1,0:T(8,128)(2,1)S(1)}, u32[]{:S(2)}, u32[]{:S(2)}) collective-permute-start(bf16[16,2048]{1,0:T(8,128)(2,1)S(1)} %get-tuple-element.29), channel_id=1, source_target_pairs={{0,4},{4,0},{8,12},{12,8},{16,20},{20,16},{24,28},{28,24},{1,5},{5... | collective-permute-start | bytes 196616 | tf_op jit(solution)/shard_map/ppermute | solution.py:357
  34.8 4.3 %collective-permute-start.17 = (bf16[16,2048]{1,0:T(8,128)(2,1)S(1)}, bf16[16,2048]{1,0:T(8,128)(2,1)S(1)}, u32[]{:S(2)}, u32[]{:S(2)}) collective-permute-start(bf16[16,2048]{1,0:T(8,128)(2,1)S(1)} %get-tuple-element.31), channel_id=1, source_target_pairs={{0,4},{4,0},{8,12},{12,8},{16,20},{20,16},{24,28},{28,24},{1,5},{5... | collective-permute-start | bytes 196616 | tf_op jit(solution)/shard_map/ppermute | solution.py:357
  34.9 6.9 %collective-permute-start.16 = (bf16[16,2048]{1,0:T(8,128)(2,1)S(1)}, bf16[16,2048]{1,0:T(8,128)(2,1)S(1)}, u32[]{:S(2)}, u32[]{:S(2)}) collective-permute-start(bf16[16,2048]{1,0:T(8,128)(2,1)S(1)} %get-tuple-element.30), channel_id=1, source_target_pairs={{0,2},{1,3},{2,0},{3,1},{4,7},{5,6},{6,5},{7,4},{8,10},{9,11},{10,... | collective-permute-start | bytes 196616 | tf_op jit(solution)/shard_map/ppermute | solution.py:352
  37.5 6.0 %collective-permute-start.19 = (bf16[16,2048]{1,0:T(8,128)(2,1)S(1)}, bf16[16,2048]{1,0:T(8,128)(2,1)S(1)}, u32[]{:S(2)}, u32[]{:S(2)}) collective-permute-start(bf16[16,2048]{1,0:T(8,128)(2,1)S(1)} %shard_map.119), channel_id=1, source_target_pairs={{0,1},{1,0},{2,3},{3,2},{4,5},{5,4},{6,7},{7,6},{8,9},{9,8},{10,11... | collective-permute-start | bytes 196616 | tf_op jit(solution)/shard_map/ppermute | solution.py:357
  39.1 6.1 %collective-permute-start.18 = (bf16[16,2048]{1,0:T(8,128)(2,1)S(1)}, bf16[16,2048]{1,0:T(8,128)(2,1)S(1)}, u32[]{:S(2)}, u32[]{:S(2)}) collective-permute-start(bf16[16,2048]{1,0:T(8,128)(2,1)S(1)} %collective-permute-done.17), channel_id=1, source_target_pairs={{0,3},{1,2},{2,1},{3,0},{4,6},{5,7},{6,4},{7,5},{8,11},{9,10},{10,... | collective-permute-start | bytes 196616 | tf_op jit(solution)/shard_map/ppermute | solution.py:352
  (4 other events, 7.4 us)
where the time goes:
time: 46 us; the launch traced here: 45.9 us
  starting transfers between devices  13.9 us (30%)
  Pallas kernels  13.8 us (30%)
  waiting for transfers between devices  13.2 us (29%)
  local copies, waits for them, and re-layouts  3.49 us (8%)
  between operations  1.47 us (3%)
    ppermute x18, starting transfers between devices, swap(): return lax.ppermute(value, axis, [(i, i ^ mask) for i in range(size)])  10.7 us
    ppermute x18, waiting for transfers between devices, swap(): return lax.ppermute(value, axis, [(i, i ^ mask) for i in range(size)])  9.4 us
    ppermute x2, waiting for transfers between devices, send_block(): return lax.ppermute(value, ('group', 'tp'), pairs)  3.79 us
    unnamed x16, local copies, waits for them, and re-layouts  3.49 us
    pallas_call x1, Pallas kernels, step(): call(lambda *refs, taken=taken: slot_kernel(*refs, groups=groups, kv_head...  3.47 us
    pallas_call x1, Pallas kernels, step(): call(lambda *refs: combine_kernel(*refs, groups=groups, slots=slots, **se...  3.44 us
    ppermute x2, starting transfers between devices, send_block(): return lax.ppermute(value, ('group', 'tp'), pairs)  3.22 us
    pallas_call x1, Pallas kernels, step(): call(lambda *refs, taken=taken: local_kernel(*refs, kv_heads=kv_heads, pi...  2.41 us
  transfers between devices with their start and end apart: 20, of which 10 were waited for; matrix products, arithmetic and copies ran while one was open for 0% of the time, Pallas kernels for 12%

commit v1 on v0

--- a/solution.py
+++ b/solution.py
@@ -10,7 +10,6 @@
 
 HEAD_DIM = 128
 LANES = 128
-PARTS = 4
 far_below = -1e30
 
 
@@ -99,7 +98,7 @@
 
     @region
     def _():
-        pipeline((score, weigh, mix), rows, 3)
+        pipeline((score, weigh, mix), rows, 4)
 
     for copy in weight_copies:
         copy.wait()
@@ -117,11 +116,11 @@
 
 
 def piece_of(weight, piece, columns):
-    step, part = piece
+    step, half = piece
     place = jnp.bitwise_xor(lax.axis_index("tp"), step_mask(lax.axis_index("group"), step))
-    depth = weight.shape[0] // PARTS
+    depth = weight.shape[0] // 2
     return weight.at[
-        pl.ds(part * depth, depth), pl.ds(pl.multiple_of(place * columns, columns), columns)
+        pl.ds(half * depth, depth), pl.ds(pl.multiple_of(place * columns, columns), columns)
     ]
 
 
@@ -236,16 +235,13 @@
         copy.wait()
 
 
-def project(x, held, same, other, chunk, own=None):
-    rows, depth = x.shape[0] // 2, x.shape[1] // PARTS
+def project(x, halves, same, other, chunk, own=None):
+    rows, depth = x.shape[0] // 2, x.shape[1] // 2
     for c in range(0, same.shape[1], chunk):
         at = slice(c, c + chunk)
-        product = sum(
-            jnp.dot(
-                x[:, p * depth : (p + 1) * depth], held[p][:, at], preferred_element_type=f32
-            )
-            for p in range(PARTS)
-        )
+        product = jnp.dot(
+            x[:, :depth], halves[0][:, at], preferred_element_type=f32
+        ) + jnp.dot(x[:, depth:], halves[1][:, at], preferred_element_type=f32)
         same[:, at] = product[:rows].astype(same.dtype)
         other[:, at] = product[rows:].astype(other.dtype)
         if own is not None:
@@ -253,9 +249,8 @@
 
 
 def combine_kernel(*refs, groups, rows, heads, slots, pieces, last, columns, chunk):
-    local, gathered = refs[:2], refs[2 : 2 + groups]
-    held, refs = refs[2 + groups : 2 + groups + PARTS], refs[2 + groups + PARTS :]
-    weight_in, x_ref, free_total, same, other, *rest = refs
+    local, gathered, halves = refs[:2], refs[2 : 2 + groups], refs[2 + groups : 4 + groups]
+    weight_in, x_ref, free_total, same, other, *rest = refs[4 + groups :]
     own = rest.pop(0) if last else None
     mixed, high, total, sems = rest[len(pieces) :]
     copies = fetch(weight_in, pieces, rest, sems, columns)
@@ -307,18 +302,18 @@
 
     @region
     def _():
-        project(x_ref[...], held, same, other, chunk, own)
+        project(x_ref[...], halves, same, other, chunk, own)
 
     for copy in copies:
         copy.wait()
 
 
 def project_kernel(x_ref, *refs, pieces, last, columns, chunk):
-    held = refs[:PARTS]
-    weight_in, same, other, *rest = refs[PARTS:]
+    halves = refs[:2]
+    weight_in, same, other, *rest = refs[2:]
     own = rest.pop(0) if last else None
     copies = fetch(weight_in, pieces, rest, rest[-1], columns)
-    region(lambda: project(x_ref[...], held, same, other, chunk, own))
+    region(lambda: project(x_ref[...], halves, same, other, chunk, own))
     for copy in copies:
         copy.wait()
 
@@ -387,7 +382,7 @@
     kv_heads = cache_keys.shape[2] // HEAD_DIM
     slots, positions = pool_keys.shape[:2]
     columns = out_weight.shape[1] // tp
-    chunk = math.gcd(columns, 512)
+    chunk = math.gcd(columns, 2048)
     sizes = dict(rows=rows, heads=heads)
 
     shards = gather_group(queries)
@@ -395,9 +390,9 @@
     copies = pltpu.SemaphoreType.DMA
 
     order = list(range(tp // 2 - 1, -1, -1))
-    pieces = [(step, part) for step in order for part in range(PARTS)]
-    held = jax.ShapeDtypeStruct((width // PARTS, columns), out_weight.dtype)
-    piece_bytes = 2 * width * columns // PARTS
+    pieces = [(step, half) for step in order for half in range(2)]
+    held = jax.ShapeDtypeStruct((width // 2, columns), out_weight.dtype)
+    piece_bytes = width * columns
     weights = {}
 
     def take(count):
@@ -408,7 +403,7 @@
     token = call(open_kernel, jax.ShapeDtypeStruct((8, LANES), f32), [HBM], vmem=1 << 20)(
         out_weight
     )
-    taken = take(0)
+    taken = take(1)
     local, *more = call(
         lambda *refs, taken=taken: local_kernel(
             *refs, kv_heads=kv_heads, pieces=taken, columns=columns, **sizes
@@ -430,7 +425,7 @@
     weights.update(zip(taken, more))
     pair_local = swap(local, "group", 1)
 
-    taken = take(3)
+    taken = take(1)
     packed, *more = call(
         lambda *refs, taken=taken: slot_kernel(
             *refs,
@@ -448,7 +443,7 @@
             pltpu.VMEM((slots * heads, HEAD_DIM), f32),
             pltpu.VMEM((slots, heads, positions), f32),
             pltpu.VMEM((slots, heads, positions), bf16),
-            copies((len(taken),)),
+            copies((1,)),
         ],
         moved=2 * (pool_keys.size + pool_values.size),
         vmem=4 << 20,
@@ -456,13 +451,13 @@
     weights.update(zip(taken, more))
 
     far = gather_group(packed)
-    taken = take(2)
+    taken = take(1)
     more = call(
         lambda *refs, taken=taken: fetch_kernel(*refs, pieces=taken, columns=columns),
         [held] * len(taken),
         [HBM, pl.BlockSpec(memory_space=pl.ANY)],
-        scratch=[copies((len(taken),))],
-        moved=piece_bytes * len(taken),
+        scratch=[copies((1,))],
+        moved=piece_bytes,
         vmem=1 << 20,
     )(out_weight, packed)
     weights.update(zip(taken, more))
@@ -472,11 +467,11 @@
     received = []
     for i, step in enumerate(order):
         last = step == 0
-        taken = take(max(0, len(pieces) - PARTS * (len(order) - 2 - i)))
+        taken = take(max(0, len(pieces) - 2 * (len(order) - 2 - i)))
         outs = [block] * 2 + [whole] * last + [held] * len(taken)
         settings = dict(pieces=taken, last=last, columns=columns, chunk=chunk)
-        ready = [weights[step, part] for part in range(PARTS)]
-        moved = piece_bytes * max(PARTS, len(taken))
+        halves = [weights[step, half] for half in range(2)]
+        moved = piece_bytes * max(2, len(taken))
         if i == 0:
             x, free_total, same, other, *more = call(
                 lambda *refs: combine_kernel(
@@ -487,21 +482,21 @@
                     jax.ShapeDtypeStruct((1,), jnp.int32),
                 ]
                 + outs,
-                [VMEM] * (2 + groups + PARTS) + [HBM],
+                [VMEM] * (4 + groups) + [HBM],
                 out_specs=[VMEM, SMEM] + [VMEM] * len(outs),
                 scratch=[pltpu.VMEM((2 * rows * heads, LANES), f32)] * 3
                 + [copies((max(1, len(taken)),))],
                 moved=moved,
-            )(local, pair_local, *far, *ready, out_weight)
+            )(local, pair_local, *far, *halves, out_weight)
         else:
             same, other, *more = call(
                 lambda *refs, settings=settings: project_kernel(*refs, **settings),
                 outs,
-                [VMEM] * (1 + PARTS) + [HBM],
+                [VMEM] * 3 + [HBM],
                 scratch=[copies((max(1, len(taken)),))],
                 moved=moved,
                 vmem=4 << 20,
-            )(x, *ready, out_weight)
+            )(x, *halves, out_weight)
         if last:
             own = more.pop(0)
         weights.update(zip(taken, more))

time: 46 us -> 45.2 us (0.983)
  Pallas kernels: 13.8 us -> 13 us
    pallas_call x1, Pallas kernels: 3.47 us -> 2.76 us  [step(): call(lambda *refs, taken=taken: slot_kernel(*refs, groups=groups, kv_head...]
    pallas_call x1, Pallas kernels: 3.44 us -> 2.74 us  [step(): call(lambda *refs: combine_kernel(*refs, groups=groups, slots=slots, **se...]
    pallas_call x1, Pallas kernels: 2.41 us -> 3.04 us  [step(): call(lambda *refs, taken=taken: local_kernel(*refs, kv_heads=kv_heads, pi...]
  transfers between devices with their start and end apart: 20 -> 20, of which waited for: 10 -> 10; matrix products, arithmetic and copies ran while one was open for 0% -> 0% of each run, Pallas kernels for 12% -> 11%
where the time goes in v1:
time: 45.2 us; the launch traced here: 45 us
  starting transfers between devices  13.9 us (31%)
  waiting for transfers between devices  13.1 us (29%)
  Pallas kernels  13 us (29%)
  local copies, waits for them, and re-layouts  3.48 us (8%)
  between operations  1.48 us (3%)
    ppermute x18, starting transfers between devices, swap(): return lax.ppermute(value, axis, [(i, i ^ mask) for i in range(size)])  10.8 us
    ppermute x18, waiting for transfers between devices, swap(): return lax.ppermute(value, axis, [(i, i ^ mask) for i in range(size)])  9.42 us
    ppermute x2, waiting for transfers between devices, send_block(): return lax.ppermute(value, ('group', 'tp'), pairs)  3.72 us
    unnamed x16, local copies, waits for them, and re-layouts  3.48 us
    ppermute x2, starting transfers between devices, send_block(): return lax.ppermute(value, ('group', 'tp'), pairs)  3.07 us
    pallas_call x1, Pallas kernels, step(): call(lambda *refs, taken=taken: local_kernel(*refs, kv_heads=kv_heads, pi...  3.04 us
    pallas_call x1, Pallas kernels, step(): call(lambda *refs, taken=taken: slot_kernel(*refs, groups=groups, kv_head...  2.76 us
    pallas_call x1, Pallas kernels, step(): call(lambda *refs: combine_kernel(*refs, groups=groups, slots=slots, **se...  2.74 us
  transfers between devices with their start and end apart: 20, of which 10 were waited for; matrix products, arithmetic and copies ran while one was open for 0% of the time, Pallas kernels for 11%

profile of v1, /device:TPU:0, one launch (start us, length us, event | category | flops | bytes accessed | tf_op | source)
XLA Modules:
  0.0 45.0 jit_solution(2244497189419269510)
XLA Ops:
  0.7 0.8 %copy-done.4 = bf16[16,2048]{1,0:T(8,128)(2,1)S(1)} copy-done((bf16[16,2048]{1,0:T(8,128)(2,1)S(1)}, bf16[16,2048]{1,0:T(8,128)(2,1)}, u32[]{:S(2)}) %copy-start.4) | copy-done | bytes 65560
  1.5 1.4 %copy-done = bf16[16,512,256]{2,1,0:T(8,128)(2,1)S(1)} copy-done((bf16[16,512,256]{2,1,0:T(8,128)(2,1)S(1)}, bf16[16,512,256]{2,1,0:T(8,128)(2,1)}, u32[]{:S(2)}) %copy-start) | copy-done | bytes 4194328
  2.9 1.3 %copy-done.1 = bf16[16,512,256]{2,1,0:T(8,128)(2,1)S(1)} copy-done((bf16[16,512,256]{2,1,0:T(8,128)(2,1)S(1)}, bf16[16,512,256]{2,1,0:T(8,128)(2,1)}, u32[]{:S(2)}) %copy-start.1) | copy-done | bytes 4194328
  4.2 3.0 %shard_map.114 = (f32[768,128]{1,0:T(8,128)S(1)}, bf16[1024,2048]{1,0:T(8,128)(2,1)S(1)}) custom-call(s32[16]{0:T(128)S(1)} %copy-done.5, bf16[16,2048]{1,0:T(8,128)(2,1)S(1)} %copy-done.4, bf16[16,512,256]{2,1,0:T(8,128)(2,1)S(1)} %copy-done, bf16[16,512,256]{2,1,0:T(8,128)(2,1)S(1)} %copy-done.1, bf16[2048,8192]{1,0:T(8,128)(2,1)} %refs_3_.5, ...), custom_call_target="tpu_custom_call" | custom-call | bytes 8388608 | tf_op jit(solution)/shard_map/pallas_call | solution.py:407
  7.8 2.6 %collective-permute-start.2 = (bf16[16,2048]{1,0:T(8,128)(2,1)S(1)}, bf16[16,2048]{1,0:T(8,128)(2,1)S(1)}, u32[]{:S(2)}, u32[]{:S(2)}) collective-permute-start(bf16[16,2048]{1,0:T(8,128)(2,1)S(1)} %copy-done.4), channel_id=1, source_target_pairs={{0,8},{4,12},{8,0},{12,4},{16,24},{20,28},{24,16},{28,20},{1,9},{5... | collective-permute-start | bytes 196616 | tf_op jit(solution)/shard_map/ppermute | solution.py:352
  10.3 1.5 %collective-permute-start.4 = (bf16[16,2048]{1,0:T(8,128)(2,1)S(1)}, bf16[16,2048]{1,0:T(8,128)(2,1)S(1)}, u32[]{:S(2)}, u32[]{:S(2)}) collective-permute-start(bf16[16,2048]{1,0:T(8,128)(2,1)S(1)} %copy-done.4), channel_id=1, source_target_pairs={{0,16},{4,20},{8,24},{12,28},{16,0},{20,4},{24,8},{28,12},{1,17},{... | collective-permute-start | bytes 196616 | tf_op jit(solution)/shard_map/ppermute | solution.py:352
  11.9 1.1 %collective-permute-done.2.refs_5_ = bf16[16,2048]{1,0:T(8,128)(2,1)S(1)} collective-permute-done((bf16[16,2048]{1,0:T(8,128)(2,1)S(1)}, bf16[16,2048]{1,0:T(8,128)(2,1)S(1)}, u32[]{:S(2)}, u32[]{:S(2)}) %collective-permute-start.2) | collective-permute-done | bytes 65568 | tf_op jit(solution)/shard_map/ppermute | solution.py:352
  13.0 1.6 %collective-permute-done.4.refs_7_ = bf16[16,2048]{1,0:T(8,128)(2,1)S(1)} collective-permute-done((bf16[16,2048]{1,0:T(8,128)(2,1)S(1)}, bf16[16,2048]{1,0:T(8,128)(2,1)S(1)}, u32[]{:S(2)}, u32[]{:S(2)}) %collective-permute-start.4) | collective-permute-done | bytes 65568 | tf_op jit(solution)/shard_map/ppermute | solution.py:352
  14.6 2.4 %collective-permute-done.6.refs_9_ = bf16[16,2048]{1,0:T(8,128)(2,1)S(1)} collective-permute-done((bf16[16,2048]{1,0:T(8,128)(2,1)S(1)}, bf16[16,2048]{1,0:T(8,128)(2,1)S(1)}, u32[]{:S(2)}, u32[]{:S(2)}) %collective-permute-start.6) | collective-permute-done | bytes 65568 | tf_op jit(solution)/shard_map/ppermute | solution.py:352
  18.3 2.8 %shard_map.115 = (bf16[48,128]{1,0:T(8,128)(2,1)S(1)}, bf16[1024,2048]{1,0:T(8,128)(2,1)S(1)}) custom-call(s32[2]{0:T(128)S(1)} %copy-done.6, s32[2]{0:T(128)S(1)} %copy-done.7, s32[1]{0:T(128)S(6)} %copy.12.refs_2_, bf16[16,2048]{1,0:T(8,128)(2,1)S(1)} %copy-done.4, bf16[16,2048]{1,0:T(8,128)(2,1)S(1)} %collective-permute-done.1.refs_4_, ...), custom_call_target="tpu_custom_call" | custom-call | bytes 8388608 | tf_op jit(solution)/shard_map/pallas_call | solution.py:429
  21.0 0.6 %collective-permute-start.9 = (bf16[48,128]{1,0:T(8,128)(2,1)S(1)}, bf16[48,128]{1,0:T(8,128)(2,1)S(1)}, u32[]{:S(2)}, u32[]{:S(2)}) collective-permute-start(bf16[48,128]{1,0:T(8,128)(2,1)S(1)} %get-tuple-element.15.refs_2_.refs_1_), channel_id=1, source_target_pairs={{0,8},{4,12},{8,0},{12,4},{16,24},{20,28},{24,16},{28,20},{1,9},{5... | collective-permute-start | bytes 36872 | tf_op jit(solution)/shard_map/ppermute | solution.py:352
  21.6 0.7 %collective-permute-start.11 = (bf16[48,128]{1,0:T(8,128)(2,1)S(1)}, bf16[48,128]{1,0:T(8,128)(2,1)S(1)}, u32[]{:S(2)}, u32[]{:S(2)}) collective-permute-start(bf16[48,128]{1,0:T(8,128)(2,1)S(1)} %get-tuple-element.15.refs_2_.refs_1_), channel_id=1, source_target_pairs={{0,16},{4,20},{8,24},{12,28},{16,0},{20,4},{24,8},{28,12},{1,17},{... | collective-permute-start | bytes 36872 | tf_op jit(solution)/shard_map/ppermute | solution.py:352
  22.3 2.3 %collective-permute-start.13 = (bf16[48,128]{1,0:T(8,128)(2,1)S(1)}, bf16[48,128]{1,0:T(8,128)(2,1)S(1)}, u32[]{:S(2)}, u32[]{:S(2)}) collective-permute-start(bf16[48,128]{1,0:T(8,128)(2,1)S(1)} %get-tuple-element.15.refs_2_.refs_1_), channel_id=1, source_target_pairs={{0,24},{4,28},{8,16},{12,20},{16,8},{20,12},{24,0},{28,4},{1,25},{... | collective-permute-start | bytes 36872 | tf_op jit(solution)/shard_map/ppermute | solution.py:352
  25.3 1.6 %collective-permute-done.13.refs_8_ = bf16[48,128]{1,0:T(8,128)(2,1)S(1)} collective-permute-done((bf16[48,128]{1,0:T(8,128)(2,1)S(1)}, bf16[48,128]{1,0:T(8,128)(2,1)S(1)}, u32[]{:S(2)}, u32[]{:S(2)}) %collective-permute-start.13) | collective-permute-done | bytes 12320 | tf_op jit(solution)/shard_map/ppermute | solution.py:352
  26.9 2.2 %shard_map.117.refs_1_ = bf16[1024,2048]{1,0:T(8,128)(2,1)S(1)} custom-call(bf16[2048,8192]{1,0:T(8,128)(2,1)} %refs_3_.5, bf16[48,128]{1,0:T(8,128)(2,1)S(1)} %get-tuple-element.15.refs_2_.refs_1_), custom_call_target="tpu_custom_call" | custom-call | bytes 4194304 | tf_op jit(solution)/shard_map/pallas_call | solution.py:455
  29.2 2.7 %shard_map.116 = (bf16[32,2048]{1,0:T(8,128)(2,1)S(1)}, s32[1]{0:T(128)}, bf16[16,2048]{1,0:T(8,128)(2,1)S(1)}, bf16[16,2048]{1,0:T(8,128)(2,1)S(1)}, bf16[1024,2048]{1,0:T(8,128)(2,1)S(1)}) custom-call(f32[768,128]{1,0:T(8,128)S(1)} %get-tuple-element.14.refs_0_, f32[768,128]{1,0:T(8,128)S(1)} %collective-permute-done.refs_1_, ...), custom_call_target="tpu_custom_call" | custom-call | bytes 8388608 | tf_op jit(solution)/shard_map/pallas_call | solution.py:476
  31.9 1.6 %shard_map.118 = (bf16[16,2048]{1,0:T(8,128)(2,1)S(1)}, bf16[16,2048]{1,0:T(8,128)(2,1)S(1)}, f32[16,2048]{1,0:T(8,128)S(1)}) custom-call(bf16[32,2048]{1,0:T(8,128)(2,1)S(1)} %get-tuple-element.18.refs_0_, bf16[1024,2048]{1,0:T(8,128)(2,1)S(1)} %shard_map.117.refs_1_, bf16[1024,2048]{1,0:T(8,128)(2,1)S(1)} %get-tuple-element.19.refs_2_, ...), custom_call_target="tpu_custom_call" | custom-call | bytes 8388608 | tf_op jit(solution)/shard_map/pallas_call | solution.py:492
  34.1 2.4 %collective-permute-start.16 = (bf16[16,2048]{1,0:T(8,128)(2,1)S(1)}, bf16[16,2048]{1,0:T(8,128)(2,1)S(1)}, u32[]{:S(2)}, u32[]{:S(2)}) collective-permute-start(bf16[16,2048]{1,0:T(8,128)(2,1)S(1)} %get-tuple-element.22), channel_id=1, source_target_pairs={{0,2},{1,3},{2,0},{3,1},{4,7},{5,6},{6,5},{7,4},{8,10},{9,11},{10,... | collective-permute-start | bytes 196616 | tf_op jit(solution)/shard_map/ppermute | solution.py:347
  36.6 1.6 %collective-permute-start.19 = (bf16[16,2048]{1,0:T(8,128)(2,1)S(1)}, bf16[16,2048]{1,0:T(8,128)(2,1)S(1)}, u32[]{:S(2)}, u32[]{:S(2)}) collective-permute-start(bf16[16,2048]{1,0:T(8,128)(2,1)S(1)} %shard_map.119), channel_id=1, source_target_pairs={{0,1},{1,0},{2,3},{3,2},{4,5},{5,4},{6,7},{7,6},{8,9},{9,8},{10,11... | collective-permute-start | bytes 196616 | tf_op jit(solution)/shard_map/ppermute | solution.py:352
  38.2 0.6 %collective-permute-start.18 = (bf16[16,2048]{1,0:T(8,128)(2,1)S(1)}, bf16[16,2048]{1,0:T(8,128)(2,1)S(1)}, u32[]{:S(2)}, u32[]{:S(2)}) collective-permute-start(bf16[16,2048]{1,0:T(8,128)(2,1)S(1)} %collective-permute-done.17), channel_id=1, source_target_pairs={{0,3},{1,2},{2,1},{3,0},{4,6},{5,7},{6,4},{7,5},{8,11},{9,10},{10,... | collective-permute-start | bytes 196616 | tf_op jit(solution)/shard_map/ppermute | solution.py:347
  38.9 1.9 %collective-permute-done.16.refs_0_ = bf16[16,2048]{1,0:T(8,128)(2,1)S(1)} collective-permute-done((bf16[16,2048]{1,0:T(8,128)(2,1)S(1)}, bf16[16,2048]{1,0:T(8,128)(2,1)S(1)}, u32[]{:S(2)}, u32[]{:S(2)}) %collective-permute-start.16) | collective-permute-done | bytes 65568 | tf_op jit(solution)/shard_map/ppermute | solution.py:347
  40.8 1.7 %collective-permute-done.19.refs_2_ = bf16[16,2048]{1,0:T(8,128)(2,1)S(1)} collective-permute-done((bf16[16,2048]{1,0:T(8,128)(2,1)S(1)}, bf16[16,2048]{1,0:T(8,128)(2,1)S(1)}, u32[]{:S(2)}, u32[]{:S(2)}) %collective-permute-start.19) | collective-permute-done | bytes 65568 | tf_op jit(solution)/shard_map/ppermute | solution.py:352
  42.5 1.8 %collective-permute-done.18.refs_1_ = bf16[16,2048]{1,0:T(8,128)(2,1)S(1)} collective-permute-done((bf16[16,2048]{1,0:T(8,128)(2,1)S(1)}, bf16[16,2048]{1,0:T(8,128)(2,1)S(1)}, u32[]{:S(2)}, u32[]{:S(2)}) %collective-permute-start.18) | collective-permute-done | bytes 65568 | tf_op jit(solution)/shard_map/ppermute | solution.py:347
  44.3 0.7 %shard_map.120 = bf16[16,2048]{1,0:T(8,128)(2,1)} custom-call(f32[16,2048]{1,0:T(8,128)S(1)} %get-tuple-element.20.own, bf16[16,2048]{1,0:T(8,128)(2,1)S(1)} %collective-permute-done.15.even.crossed, bf16[16,2048]{1,0:T(8,128)(2,1)S(1)} %collective-permute-done.16.refs_0_, bf16[16,2048]{1,0:T(8,128)(2,1)S(1)} %collective-permute-done.18.refs_1_, ...), custom_call_target="tpu_custom_call" | custom-call | tf_op jit(solution)/shard_map/pallas_call | solution.py:510
  (40 shorter events, 2.6 us)
Async XLA Ops:
  4.1 14.1 %copy-start.2 = (bf16[2,4096,256]{2,1,0:T(8,128)(2,1)S(1)}, bf16[2,4096,256]{2,1,0:T(8,128)(2,1)}, u32[]{:S(2)}) copy-start(bf16[2,4096,256]{2,1,0:T(8,128)(2,1)} %refs_11_.1) | copy-start | bytes 12582916
  4.1 14.1 %copy-start.3 = (bf16[2,4096,256]{2,1,0:T(8,128)(2,1)S(1)}, bf16[2,4096,256]{2,1,0:T(8,128)(2,1)}, u32[]{:S(2)}) copy-start(bf16[2,4096,256]{2,1,0:T(8,128)(2,1)} %refs_12_.2) | copy-start | bytes 12582916
  4.1 14.1 %copy-start.6 = (s32[2]{0:T(128)S(1)}, s32[2]{0:T(128)}, u32[]{:S(2)}) copy-start(s32[2]{0:T(128)} %refs_0_.4) | copy-start | bytes 28
  4.1 14.1 %copy-start.7 = (s32[2]{0:T(128)S(1)}, s32[2]{0:T(128)}, u32[]{:S(2)}) copy-start(s32[2]{0:T(128)} %refs_1_.3) | copy-start | bytes 28
  7.2 22.0 %collective-permute-start = (f32[768,128]{1,0:T(8,128)S(1)}, f32[768,128]{1,0:T(8,128)S(1)}, u32[]{:S(2)}, u32[]{:S(2)}) collective-permute-start(f32[768,128]{1,0:T(8,128)S(1)} %get-tuple-element.14.refs_0_), channel_id=1, source_target_pairs={{0,4},{4,0},{8,12},{12,8},{16,20},{20,16},{24,28},{28,24},{1,5},{5... | collective-permute-start | bytes 1179656 | tf_op jit(solution)/shard_map/ppermute | solution.py:352
  7.8 5.2 %collective-permute-start.2 = (bf16[16,2048]{1,0:T(8,128)(2,1)S(1)}, bf16[16,2048]{1,0:T(8,128)(2,1)S(1)}, u32[]{:S(2)}, u32[]{:S(2)}) collective-permute-start(bf16[16,2048]{1,0:T(8,128)(2,1)S(1)} %copy-done.4), channel_id=1, source_target_pairs={{0,8},{4,12},{8,0},{12,4},{16,24},{20,28},{24,16},{28,20},{1,9},{5... | collective-permute-start | bytes 196616 | tf_op jit(solution)/shard_map/ppermute | solution.py:352
  10.3 4.3 %collective-permute-start.4 = (bf16[16,2048]{1,0:T(8,128)(2,1)S(1)}, bf16[16,2048]{1,0:T(8,128)(2,1)S(1)}, u32[]{:S(2)}, u32[]{:S(2)}) collective-permute-start(bf16[16,2048]{1,0:T(8,128)(2,1)S(1)} %copy-done.4), channel_id=1, source_target_pairs={{0,16},{4,20},{8,24},{12,28},{16,0},{20,4},{24,8},{28,12},{1,17},{... | collective-permute-start | bytes 196616 | tf_op jit(solution)/shard_map/ppermute | solution.py:352
  11.8 5.2 %collective-permute-start.6 = (bf16[16,2048]{1,0:T(8,128)(2,1)S(1)}, bf16[16,2048]{1,0:T(8,128)(2,1)S(1)}, u32[]{:S(2)}, u32[]{:S(2)}) collective-permute-start(bf16[16,2048]{1,0:T(8,128)(2,1)S(1)} %copy-done.4), channel_id=1, source_target_pairs={{0,24},{4,28},{8,16},{12,20},{16,8},{20,12},{24,0},{28,4},{1,25},{... | collective-permute-start | bytes 196616 | tf_op jit(solution)/shard_map/ppermute | solution.py:352
  11.9 5.8 %collective-permute-start.1 = (bf16[16,2048]{1,0:T(8,128)(2,1)S(1)}, bf16[16,2048]{1,0:T(8,128)(2,1)S(1)}, u32[]{:S(2)}, u32[]{:S(2)}) collective-permute-start(bf16[16,2048]{1,0:T(8,128)(2,1)S(1)} %copy-done.4), channel_id=1, source_target_pairs={{0,4},{4,0},{8,12},{12,8},{16,20},{20,16},{24,28},{28,24},{1,5},{5... | collective-permute-start | bytes 196616 | tf_op jit(solution)/shard_map/ppermute | solution.py:352
  13.0 4.7 %collective-permute-start.3 = (bf16[16,2048]{1,0:T(8,128)(2,1)S(1)}, bf16[16,2048]{1,0:T(8,128)(2,1)S(1)}, u32[]{:S(2)}, u32[]{:S(2)}) collective-permute-start(bf16[16,2048]{1,0:T(8,128)(2,1)S(1)} %collective-permute-done.2.refs_5_), channel_id=1, source_target_pairs={{0,4},{4,0},{8,12},{12,8},{16,20},{20,16},{24,28},{28,24},{1,5},{5... | collective-permute-start | bytes 196616 | tf_op jit(solution)/shard_map/ppermute | solution.py:352
  14.6 3.1 %collective-permute-start.5 = (bf16[16,2048]{1,0:T(8,128)(2,1)S(1)}, bf16[16,2048]{1,0:T(8,128)(2,1)S(1)}, u32[]{:S(2)}, u32[]{:S(2)}) collective-permute-start(bf16[16,2048]{1,0:T(8,128)(2,1)S(1)} %collective-permute-done.4.refs_7_), channel_id=1, source_target_pairs={{0,4},{4,0},{8,12},{12,8},{16,20},{20,16},{24,28},{28,24},{1,5},{5... | collective-permute-start | bytes 196616 | tf_op jit(solution)/shard_map/ppermute | solution.py:352
  17.0 1.3 %collective-permute-start.7 = (bf16[16,2048]{1,0:T(8,128)(2,1)S(1)}, bf16[16,2048]{1,0:T(8,128)(2,1)S(1)}, u32[]{:S(2)}, u32[]{:S(2)}) collective-permute-start(bf16[16,2048]{1,0:T(8,128)(2,1)S(1)} %collective-permute-done.6.refs_9_), channel_id=1, source_target_pairs={{0,4},{4,0},{8,12},{12,8},{16,20},{20,16},{24,28},{28,24},{1,5},{5... | collective-permute-start | bytes 196616 | tf_op jit(solution)/shard_map/ppermute | solution.py:352
  21.0 3.8 %collective-permute-start.9 = (bf16[48,128]{1,0:T(8,128)(2,1)S(1)}, bf16[48,128]{1,0:T(8,128)(2,1)S(1)}, u32[]{:S(2)}, u32[]{:S(2)}) collective-permute-start(bf16[48,128]{1,0:T(8,128)(2,1)S(1)} %get-tuple-element.15.refs_2_.refs_1_), channel_id=1, source_target_pairs={{0,8},{4,12},{8,0},{12,4},{16,24},{20,28},{24,16},{28,20},{1,9},{5... | collective-permute-start | bytes 36872 | tf_op jit(solution)/shard_map/ppermute | solution.py:352
  21.6 3.7 %collective-permute-start.11 = (bf16[48,128]{1,0:T(8,128)(2,1)S(1)}, bf16[48,128]{1,0:T(8,128)(2,1)S(1)}, u32[]{:S(2)}, u32[]{:S(2)}) collective-permute-start(bf16[48,128]{1,0:T(8,128)(2,1)S(1)} %get-tuple-element.15.refs_2_.refs_1_), channel_id=1, source_target_pairs={{0,16},{4,20},{8,24},{12,28},{16,0},{20,4},{24,8},{28,12},{1,17},{... | collective-permute-start | bytes 36872 | tf_op jit(solution)/shard_map/ppermute | solution.py:352
  22.3 4.6 %collective-permute-start.13 = (bf16[48,128]{1,0:T(8,128)(2,1)S(1)}, bf16[48,128]{1,0:T(8,128)(2,1)S(1)}, u32[]{:S(2)}, u32[]{:S(2)}) collective-permute-start(bf16[48,128]{1,0:T(8,128)(2,1)S(1)} %get-tuple-element.15.refs_2_.refs_1_), channel_id=1, source_target_pairs={{0,24},{4,28},{8,16},{12,20},{16,8},{20,12},{24,0},{28,4},{1,25},{... | collective-permute-start | bytes 36872 | tf_op jit(solution)/shard_map/ppermute | solution.py:352
  24.6 4.5 %collective-permute-start.8 = (bf16[48,128]{1,0:T(8,128)(2,1)S(1)}, bf16[48,128]{1,0:T(8,128)(2,1)S(1)}, u32[]{:S(2)}, u32[]{:S(2)}) collective-permute-start(bf16[48,128]{1,0:T(8,128)(2,1)S(1)} %get-tuple-element.15.refs_2_.refs_1_), channel_id=1, source_target_pairs={{0,4},{4,0},{8,12},{12,8},{16,20},{20,16},{24,28},{28,24},{1,5},{5... | collective-permute-start | bytes 36872 | tf_op jit(solution)/shard_map/ppermute | solution.py:352
  24.8 4.3 %collective-permute-start.10 = (bf16[48,128]{1,0:T(8,128)(2,1)S(1)}, bf16[48,128]{1,0:T(8,128)(2,1)S(1)}, u32[]{:S(2)}, u32[]{:S(2)}) collective-permute-start(bf16[48,128]{1,0:T(8,128)(2,1)S(1)} %collective-permute-done.9.refs_4_), channel_id=1, source_target_pairs={{0,4},{4,0},{8,12},{12,8},{16,20},{20,16},{24,28},{28,24},{1,5},{5... | collective-permute-start | bytes 36872 | tf_op jit(solution)/shard_map/ppermute | solution.py:352
  25.3 3.8 %collective-permute-start.12 = (bf16[48,128]{1,0:T(8,128)(2,1)S(1)}, bf16[48,128]{1,0:T(8,128)(2,1)S(1)}, u32[]{:S(2)}, u32[]{:S(2)}) collective-permute-start(bf16[48,128]{1,0:T(8,128)(2,1)S(1)} %collective-permute-done.11.refs_6_), channel_id=1, source_target_pairs={{0,4},{4,0},{8,12},{12,8},{16,20},{20,16},{24,28},{28,24},{1,5},{5... | collective-permute-start | bytes 36872 | tf_op jit(solution)/shard_map/ppermute | solution.py:352
  26.9 2.2 %collective-permute-start.14 = (bf16[48,128]{1,0:T(8,128)(2,1)S(1)}, bf16[48,128]{1,0:T(8,128)(2,1)S(1)}, u32[]{:S(2)}, u32[]{:S(2)}) collective-permute-start(bf16[48,128]{1,0:T(8,128)(2,1)S(1)} %collective-permute-done.13.refs_8_), channel_id=1, source_target_pairs={{0,4},{4,0},{8,12},{12,8},{16,20},{20,16},{24,28},{28,24},{1,5},{5... | collective-permute-start | bytes 36872 | tf_op jit(solution)/shard_map/ppermute | solution.py:352
  33.5 3.1 %collective-permute-start.15 = (bf16[16,2048]{1,0:T(8,128)(2,1)S(1)}, bf16[16,2048]{1,0:T(8,128)(2,1)S(1)}, u32[]{:S(2)}, u32[]{:S(2)}) collective-permute-start(bf16[16,2048]{1,0:T(8,128)(2,1)S(1)} %get-tuple-element.21), channel_id=1, source_target_pairs={{0,4},{4,0},{8,12},{12,8},{16,20},{20,16},{24,28},{28,24},{1,5},{5... | collective-permute-start | bytes 196616 | tf_op jit(solution)/shard_map/ppermute | solution.py:352
  34.1 4.2 %collective-permute-start.17 = (bf16[16,2048]{1,0:T(8,128)(2,1)S(1)}, bf16[16,2048]{1,0:T(8,128)(2,1)S(1)}, u32[]{:S(2)}, u32[]{:S(2)}) collective-permute-start(bf16[16,2048]{1,0:T(8,128)(2,1)S(1)} %get-tuple-element.23), channel_id=1, source_target_pairs={{0,4},{4,0},{8,12},{12,8},{16,20},{20,16},{24,28},{28,24},{1,5},{5... | collective-permute-start | bytes 196616 | tf_op jit(solution)/shard_map/ppermute | solution.py:352
  34.1 6.7 %collective-permute-start.16 = (bf16[16,2048]{1,0:T(8,128)(2,1)S(1)}, bf16[16,2048]{1,0:T(8,128)(2,1)S(1)}, u32[]{:S(2)}, u32[]{:S(2)}) collective-permute-start(bf16[16,2048]{1,0:T(8,128)(2,1)S(1)} %get-tuple-element.22), channel_id=1, source_target_pairs={{0,2},{1,3},{2,0},{3,1},{4,7},{5,6},{6,5},{7,4},{8,10},{9,11},{10,... | collective-permute-start | bytes 196616 | tf_op jit(solution)/shard_map/ppermute | solution.py:347
  36.6 5.9 %collective-permute-start.19 = (bf16[16,2048]{1,0:T(8,128)(2,1)S(1)}, bf16[16,2048]{1,0:T(8,128)(2,1)S(1)}, u32[]{:S(2)}, u32[]{:S(2)}) collective-permute-start(bf16[16,2048]{1,0:T(8,128)(2,1)S(1)} %shard_map.119), channel_id=1, source_target_pairs={{0,1},{1,0},{2,3},{3,2},{4,5},{5,4},{6,7},{7,6},{8,9},{9,8},{10,11... | collective-permute-start | bytes 196616 | tf_op jit(solution)/shard_map/ppermute | solution.py:352
  38.2 6.1 %collective-permute-start.18 = (bf16[16,2048]{1,0:T(8,128)(2,1)S(1)}, bf16[16,2048]{1,0:T(8,128)(2,1)S(1)}, u32[]{:S(2)}, u32[]{:S(2)}) collective-permute-start(bf16[16,2048]{1,0:T(8,128)(2,1)S(1)} %collective-permute-done.17), channel_id=1, source_target_pairs={{0,3},{1,2},{2,1},{3,0},{4,6},{5,7},{6,4},{7,5},{8,11},{9,10},{10,... | collective-permute-start | bytes 196616 | tf_op jit(solution)/shard_map/ppermute | solution.py:347
  (4 other events, 10.0 us)
